TPU v7x, 512 devices: a whole 4x4x16 slice. The times are simulated.
512 devices in a mesh: ctx: 32 (over z, x_lo), zero: 16 (over x_hi, y, core).
Axes of the slice: x: 4 (x_hi: 2, x_lo: 2; x = x_hi * 2 + x_lo), y: 4, z: 16, core: 2. Of those that a mesh axis runs over, the one named last changes fastest.
Arguments:
- activations: bfloat16 [16384, 4096], P('ctx', 'zero'), may hold values from -1200 to 1200
- norm_gain: bfloat16 [4096], replicated, may hold values from 0.099609375 to 1.8984375
- query_weight: bfloat16 [4096, 4096], P('ctx', 'zero'), may hold values from -24 to 24
- kv_weight: bfloat16 [4096, 16, 128], P('ctx', 'zero'), may hold values from -1 to 1
- out_weight: bfloat16 [4096, 4096], P('zero', 'ctx'), may hold values from -0.09375 to 0.09375
- tile_mask: int32 [32, 4, 4], P('ctx'), may hold values from 0 to 1, as said below
- anchor_mask: int32 [32, 4, 4], P('ctx'), may hold values 0 or 1
- anchor_index: int32 [1], replicated, may hold values from 0 to 31
Outputs:
- mixed: bfloat16 [16384, 4096], P(('ctx', 'zero'))
Inputs may be any that keep to these rules, and one draw needn't show every extreme that they name: `tile_mask`: entries of every block's table above the diagonal are 0 and diagonal entries are 1.
All inputs are finite; a program needn't handle non-finite values. No bound on the sum of `anchor_mask` on one device may be relied on, other than what follows from the above.
Results may differ from a plain program's by a relative error of at most 0.02.
Values may be sent and summed in bfloat16 or wider, within the bound.
A program may use at most 64 MiB of HBM per device.

v0:
```python
import jax
import jax.numpy as jnp
from jax import lax
from jax.sharding import PartitionSpec as P


def from_partner(value, axis, stride):
    mask = 2**stride
    pairs = [(source, source ^ mask) for source in range(lax.axis_size(axis))]
    return lax.ppermute(value, axis, pairs)


def from_root(block, axis, holder):
    block = jnp.where(lax.axis_index(axis) == holder, block, jnp.zeros_like(block))
    return lax.psum(block, axis)


def rotate(vectors, positions):
    half_size = vectors.shape[-1] // 2
    frequency = jnp.power(
        jnp.float32(500000.0), -(jnp.arange(half_size, dtype=jnp.float32) * 2.0 / vectors.shape[-1])
    )
    angles = positions.astype(jnp.float32)[:, None] * frequency[None, :]
    cosine_table = jnp.cos(angles)[:, None, :]
    sine_table = jnp.sin(angles)[:, None, :]
    first = vectors[..., :half_size]
    second = vectors[..., half_size:]
    return jnp.concatenate(
        [first * cosine_table - second * sine_table, second * cosine_table + first * sine_table], -1
    )


def expand_tiles(table, tile_size):
    tiles = table.shape[0]
    return jnp.broadcast_to(table[:, None, :, None], (tiles, tile_size, tiles, tile_size)).reshape(
        tiles * tile_size, tiles * tile_size
    )


def local(
    activations,
    norm_gain,
    query_weight,
    kv_weight,
    out_weight,
    tile_mask,
    anchor_mask,
    anchor_index,
):
    block_rows = activations.shape[0]
    head_size = kv_weight.shape[2]
    zero_rank = lax.axis_index("zero")
    ctx_rank = lax.axis_index("ctx")
    gain_float = norm_gain.astype(jnp.float32)
    gathered = lax.all_gather(activations, "zero", axis=1, tiled=True)
    x_float = gathered.astype(jnp.float32)
    mean_square = jnp.mean(x_float * x_float, -1, keepdims=True)
    normed = (x_float * lax.rsqrt(mean_square + 1e-05) * gain_float).astype(jnp.bfloat16)
    kv_rows_local = kv_weight[:, 0, :]

    def add_one(piece_rows):
        return jnp.dot(normed, piece_rows, preferred_element_type=jnp.float32)

    query_linear = add_one(lax.all_gather(query_weight, "ctx", axis=0, tiled=True))
    kv_linear = add_one(lax.all_gather(kv_rows_local, "ctx", axis=0, tiled=True))
    positions = ctx_rank * block_rows + jnp.arange(block_rows, dtype=jnp.int32)
    queries = (
        rotate(query_linear.reshape(block_rows, -1, head_size), positions) * head_size ** (-0.5)
    ).astype(jnp.bfloat16)
    is_key = zero_rank % 2 == 0
    own_half = jnp.where(
        is_key, rotate(kv_linear[:, None, :], positions)[:, 0, :], kv_linear
    ).astype(jnp.bfloat16)
    partner = from_partner(own_half, "zero", 0)
    own_keys = jnp.where(is_key, own_half, partner)
    own_values = jnp.where(is_key, partner, own_half)
    anchor_block = anchor_index[0]
    anchor_pair = from_root(jnp.stack([own_keys, own_values]), "ctx", anchor_block)
    all_keys = jnp.concatenate([anchor_pair[0], own_keys], 0)
    all_values = jnp.concatenate([anchor_pair[1], own_values], 0)
    scores = jnp.einsum("thd,kd->htk", queries, all_keys, preferred_element_type=jnp.float32)
    tile_size = block_rows // tile_mask.shape[1]
    row_offsets = jnp.arange(block_rows, dtype=jnp.int32)
    far_visible = (expand_tiles(anchor_mask[0], tile_size) == 1) & (ctx_rank != anchor_block)
    near_visible = (expand_tiles(tile_mask[0], tile_size) == 1) & (
        row_offsets[None, :] <= row_offsets[:, None]
    )
    visible = jnp.concatenate([far_visible, near_visible], 1)[None]
    scores = jnp.where(visible, scores, jnp.float32(-1e30))
    largest = jnp.max(scores, -1, keepdims=True)
    weights = jnp.where(visible, jnp.exp(scores - largest), jnp.float32(0.0))
    row_total = jnp.sum(weights, -1)
    rounded = weights.astype(jnp.bfloat16)
    attended = (
        jnp.einsum("htk,kd->thd", rounded, all_values, preferred_element_type=jnp.float32)
        / jnp.transpose(row_total)[:, :, None]
    )
    attended = attended.astype(jnp.bfloat16).reshape(block_rows, -1)
    out_rows = lax.all_gather(out_weight, "ctx", axis=1, tiled=True)
    return lax.psum_scatter(
        jnp.dot(attended, out_rows, preferred_element_type=jnp.float32).astype(jnp.bfloat16),
        "zero",
        scatter_dimension=0,
        tiled=True,
    )


def solution(mesh):
    placed = (
        P("ctx", "zero"),
        P(),
        P("ctx", "zero"),
        P("ctx", "zero", None),
        P("zero", "ctx"),
        P("ctx", None, None),
        P("ctx", None, None),
        P(),
    )
    return jax.shard_map(
        local, mesh=mesh, in_specs=placed, out_specs=P(("ctx", "zero"), None), check_vma=False
    )
```

profile of v0, /device:TPU:1, one launch (start us, length us, event | category | flops | bytes accessed | tf_op | source)
XLA Modules:
  0.0 865.4 jit_solution(16125754676907653811)
XLA Ops:
  6.5 0.7 all-gather.6.cloned.1.call-update
  7.3 0.7 all-gather.12.cloned.1.call-update
  8.1 0.7 all-gather.8.cloned.1.call-update
  8.8 0.7 convert_element_type.33
  9.5 78.4 %all-gather.6.cloned.1.call-done = bf16[512,4096]{1,0:T(8,128)(2,1)} async-done(((bf16[512,256]{1,0:T(8,128)(2,1)}), bf16[512,4096]{1,0:T(8,128)(2,1)}) %all-gather.6.cloned.1.call-update) | async-done | bytes 4194320 | tf_op jit(solution)/shard_map/all_gather | solution.py:55
  87.9 3.1 fusion.1
  91.0 105.8 %all-gather.12.cloned.1.call-done = bf16[4096,1,128]{2,0,1:T(8,128)(2,1)} async-done(((bf16[128,1,128]{2,0,1:T(8,128)(2,1)}), bf16[4096,1,128]{2,0,1:T(8,128)(2,1)}) %all-gather.12.cloned.1.call-update) | async-done | bytes 1048592 | tf_op jit(solution)/shard_map/all_gather | solution.py:65
  196.9 4.1 fusion.17
  201.0 0.6 fusion.36
  201.6 24.4 %collective-permute-start = (bf16[512,128]{0,1:T(8,128)(2,1)S(1)}, bf16[512,128]{0,1:T(8,128)(2,1)S(1)}, u32[]{:S(2)}, u32[]{:S(2)}) collective-permute-start(bf16[512,128]{0,1:T(8,128)(2,1)S(1)} %fusion.28), channel_id=1, source_target_pairs={{0,1},{1,0},{2,3},{3,2},{4,5},{5,4},{6,7},{7,6},{8,9},{9,8},{10,11... | collective-permute-start | bytes 393224 | tf_op jit(solution)/shard_map/ppermute | solution.py:10
  226.6 0.3 collective-permute-done
  227.0 0.7 maximum_select_fusion
  227.8 0.5 all-gather.10.cloned.1.call-update
  228.4 0.1 copy.9
  228.5 0.2 broadcast_in_dim.24
  228.7 0.1 copy.24
  228.9 0.1 copy.10
  229.0 0.2 broadcast_in_dim.29
  229.2 0.1 fusion.23
  229.4 1.0 multiply_cosine_fusion
  230.4 101.1 %all-gather.8.cloned.1.call-done = bf16[4096,256]{1,0:T(8,128)(2,1)} async-done(((bf16[128,256]{1,0:T(8,128)(2,1)}), bf16[4096,256]{1,0:T(8,128)(2,1)}) %all-gather.8.cloned.1.call-update) | async-done | bytes 2097168 | tf_op jit(solution)/shard_map/all_gather | solution.py:64
  331.5 4.4 fusion.15
  335.9 0.2 copy.18
  336.1 0.2 copy.19
  336.3 0.1 multiply_subtract_fusion
  336.5 260.9 %all-reduce.2.cloned.1.call-done = bf16[2,512,128]{1,2,0:T(8,128)(2,1)} async-done(((bf16[2,512,128]{1,2,0:T(8,128)(2,1)}), bf16[2,512,128]{1,2,0:T(8,128)(2,1)}) %all-reduce.2.cloned.1.call-update) | async-done | bytes 262160 | tf_op jit(solution)/shard_map/psum | solution.py:15
  597.3 1.0 slice_bitcast_fusion.1
  598.3 3.5 fusion.45
  601.8 2.0 fusion.19
  603.9 127.0 %all-gather.10.cloned.1.call-done = bf16[256,4096]{1,0:T(8,128)(2,1)} async-done(((bf16[256,128]{1,0:T(8,128)(2,1)}), bf16[256,4096]{1,0:T(8,128)(2,1)}) %all-gather.10.cloned.1.call-update) | async-done | bytes 2097168 | tf_op jit(solution)/shard_map/all_gather | solution.py:99
  730.8 4.8 convolution_convert_fusion
  735.7 122.9 %reduce-scatter.2.cloned.1.call-done = bf16[32,4096]{1,0:T(8,128)(2,1)} async-done(((bf16[512,4096]{1,0:T(8,128)(2,1)}), bf16[32,4096]{1,0:T(8,128)(2,1)}) %reduce-scatter.2.cloned.1.call-update) | async-done | bytes 262160 | tf_op jit(solution)/shard_map/reduce_scatter | solution.py:100
  (21 shorter events, 0.4 us)
Async XLA Ops:
  6.5 81.4 %all-gather.6.cloned.1.call-start = ((), (), s32[]{:S(2)}) async-start(), calls=%async_computation.1 | async-start | bytes 4456448 | tf_op jit(solution)/shard_map/all_gather | solution.py:55
  7.3 189.6 %all-gather.12.cloned.1.call-start = ((), (), s32[]{:S(2)}) async-start(), calls=%async_computation.6 | async-start | bytes 1081344 | tf_op jit(solution)/shard_map/all_gather | solution.py:65
  8.0 323.5 %all-gather.8.cloned.1.call-start = ((), (), s32[]{:S(2)}) async-start(), calls=%async_computation.3 | async-start | bytes 2162688 | tf_op jit(solution)/shard_map/all_gather | solution.py:64
  8.7 588.6 %all-reduce.2.cloned.1.call-start = ((), (), s32[]{:S(2)}) async-start(), calls=%async_computation.2 | async-start | bytes 524288 | tf_op jit(solution)/shard_map/psum | solution.py:15
  91.0 137.3 %copy-start.1 = (s32[1,4,4]{2,1,0:T(4,128)S(1)}, s32[1,4,4]{2,1,0:T(4,128)}, u32[]{:S(2)}) copy-start(s32[1,4,4]{2,1,0:T(4,128)} %param.14) | copy-start | bytes 196
  91.0 137.8 %copy-start = (s32[1,4,4]{2,1,0:T(4,128)S(1)}, s32[1,4,4]{2,1,0:T(4,128)}, u32[]{:S(2)}) copy-start(s32[1,4,4]{2,1,0:T(4,128)} %param.13) | copy-start | bytes 196
  201.6 25.4 %collective-permute-start = (bf16[512,128]{0,1:T(8,128)(2,1)S(1)}, bf16[512,128]{0,1:T(8,128)(2,1)S(1)}, u32[]{:S(2)}, u32[]{:S(2)}) collective-permute-start(bf16[512,128]{0,1:T(8,128)(2,1)S(1)} %fusion.28), channel_id=1, source_target_pairs={{0,1},{1,0},{2,3},{3,2},{4,5},{5,4},{6,7},{7,6},{8,9},{9,8},{10,11... | collective-permute-start | bytes 393224 | tf_op jit(solution)/shard_map/ppermute | solution.py:10
  227.7 503.1 %all-gather.10.cloned.1.call-start = ((), (), s32[]{:S(2)}) async-start(), calls=%async_computation.4 | async-start | bytes 2162688 | tf_op jit(solution)/shard_map/all_gather | solution.py:99
  228.3 630.2 %reduce-scatter.2.cloned.1.call-start = ((), (), s32[]{:S(2)}) async-start(), calls=%async_computation.5 | async-start | bytes 4456448 | tf_op jit(solution)/shard_map/reduce_scatter | solution.py:100
Sparse Core Ops, SparseCore 0:
  10.5 77.4 all-gather.5
  90.0 106.8 all-gather.11
  199.0 132.4 all-gather.7
  334.2 263.0 all-reduce.1
  599.2 131.6 all-gather.9
  735.8 122.6 reduce-scatter.1
where the time goes:
time: 866 us; the launch traced here: 865 us
  waiting for transfers between devices  799 us (92%)
  starting transfers between devices  24.6 us (3%)
  matrix products  18.9 us (2%)
  between operations  14.3 us (2%)
    psum x1, waiting for transfers between devices, from_root(): return lax.psum(block, axis)  261 us
    all_gather x1, waiting for transfers between devices, local(): out_rows = lax.all_gather(out_weight, 'ctx', axis=1, tiled=True)  127 us
    reduce_scatter x1, waiting for transfers between devices, local(): lax.psum_scatter(jnp.dot(attended, out_rows, preferred_element_type=jnp.f...  123 us
    all_gather x1, waiting for transfers between devices, local(): lax.all_gather(kv_rows_local, 'ctx', axis=0, tiled=True)  106 us
    all_gather x1, waiting for transfers between devices, local(): lax.all_gather(query_weight, 'ctx', axis=0, tiled=True)  101 us
    all_gather x1, waiting for transfers between devices, local(): gathered = lax.all_gather(activations, 'zero', axis=1, tiled=True)  78.4 us
    ppermute x1, starting transfers between devices, from_partner(): return lax.ppermute(value, axis, pairs)  24.4 us
  transfers between devices with their start and end apart: 7, of which 7 were waited for; matrix products, arithmetic and copies ran while one was open for 3% of the time, Pallas kernels for 0%

commit v1 on v0

v1 whole, which is shorter than its diff:
```python
import functools

import numpy as np

import jax
import jax.numpy as jnp
from jax import lax
from jax.experimental import pallas as pl
from jax.experimental.pallas import tpu as pltpu
from jax.sharding import PartitionSpec as P

MESH = pl.DeviceIdType.MESH
F32 = jnp.float32
BF16 = jnp.bfloat16
MASKED = -1e30
UNITS = 8
LAG = 1

ORDER_HOME = [
    ("A", 0, 0, 0), ("A", 0, 0, 1), ("B", 0, 0, 0), ("B", 0, 0, 1), ("A", 0, 3, 0), ("A", 0, 1, 0),
    ("A", 0, 3, 1), ("A", 0, 1, 1), ("B", 0, 3, 0), ("B", 0, 1, 0), ("B", 0, 3, 1), ("B", 0, 1, 1),
    ("A", 0, 2, 0), ("A", 2, 0, 0), ("A", 2, 0, 1), ("B", 2, 0, 0), ("A", 0, 2, 1), ("B", 0, 2, 0),
    ("B", 0, 2, 1), ("B", 2, 0, 1), ("A", 2, 3, 0), ("A", 2, 1, 0), ("B", 2, 3, 0), ("B", 2, 3, 1),
    ("A", 2, 3, 1), ("A", 2, 1, 1), ("B", 2, 1, 0), ("B", 2, 1, 1), ("A", 2, 2, 0), ("A", 2, 2, 1),
    ("B", 2, 2, 0), ("B", 2, 2, 1),
]
ORDER_AWAY = [
    ("A", 1, 0, 0), ("A", 3, 0, 0), ("A", 1, 0, 1), ("A", 3, 0, 1), ("B", 1, 0, 0), ("B", 3, 0, 0),
    ("B", 1, 0, 1), ("B", 3, 0, 1), ("A", 1, 3, 0), ("A", 1, 1, 0), ("A", 3, 3, 0), ("B", 1, 3, 0),
    ("B", 3, 3, 0), ("A", 3, 1, 0), ("A", 1, 3, 1), ("B", 1, 1, 0), ("B", 3, 1, 0), ("A", 1, 1, 1),
    ("B", 3, 3, 1), ("A", 3, 3, 1), ("A", 3, 1, 1), ("B", 1, 3, 1), ("B", 3, 1, 1), ("B", 1, 1, 1),
    ("A", 1, 2, 0), ("B", 3, 2, 0), ("A", 1, 2, 1), ("B", 1, 2, 0), ("B", 3, 2, 1), ("A", 3, 2, 0),
    ("A", 3, 2, 1), ("B", 1, 2, 1),
]
STEPS = [(1, 0), (-1, 0), (0, 1), (0, -1)]
XP, XM, YP, YM = range(4)


def onward(kind, dx, dy, half):
    first, second = (dx, dy) if kind == "A" else (dy, dx)
    fp, fm, sp, sm = (XP, XM, YP, YM) if kind == "A" else (YP, YM, XP, XM)
    ways = []
    if second == 0:
        if first == 0:
            ways += [fp, fm]
        if first == 1 and half == 0:
            ways += [fp]
        if first == 3 and half == 1:
            ways += [fm]
        ways += [sp, sm]
    if second == 1 and half == 0:
        ways += [sp]
    if second == 3 and half == 1:
        ways += [sm]
    return ways


def body(
    acts, gain, wq, wkv, wo, tmask, amask, aidx, ctab, stab, coff, soff, out,
    X, WQ, WKV, WO, ACCQ, ACCK, SSQ, QB, KV, TMR, AMR, BOWN, BFAR,
    AB, CAND, AR, SEL, AKV, MS, LS, ACC, ATT, PB, RX, RYC, RYF, SB, OB,
    rx, sx, sd, loc, r0kv, r0q, r0o, s0, rz, sz, rs, ss, rm, sm,
    ra, sa, rar, sar, rak, sak, rad, sad,
    rpx, spx, rpyc, rpyf, spy, rpd, spd,
):
    ctx = lax.axis_index("ctx")
    zero = lax.axis_index("zero")
    z, xl = lax.div(ctx, 2), lax.rem(ctx, 2)
    xh, y, core = lax.div(zero, 8), lax.rem(lax.div(zero, 2), 4), lax.rem(zero, 2)
    x = 2 * xh + xl
    sib = 1 - core
    sgn = 1 - 2 * core
    home = core == xl
    away = core != xl
    pdx = 1 - 2 * xl

    def at(dx=0, dy=0, dz=0, to=None):
        nx, ny, nz = lax.rem(x + dx + 4, 4), lax.rem(y + dy + 4, 4), lax.rem(z + dz + 16, 16)
        to = core if to is None else to
        return (nz * 2 + lax.rem(nx, 2), (lax.div(nx, 2) * 4 + ny) * 2 + to)

    def remote(src, dst, send, recv, dev):
        pltpu.make_async_remote_copy(
            src_ref=src, dst_ref=dst, send_sem=send, recv_sem=recv, device_id=dev, device_id_type=MESH
        ).start()

    def wait(ref, sem):
        pltpu.make_async_copy(ref, ref, sem).wait()

    barrier = pltpu.get_barrier_semaphore()
    greet = [at(to=sib), at(dx=1), at(dx=-1), at(dx=pdx, to=sib), at(dy=1), at(dy=-1)]
    for dev in greet:
        pl.semaphore_signal(barrier, inc=1, device_id=dev, device_id_type=MESH)

    @pl.loop(1, 16)
    def _(d):
        pl.semaphore_signal(barrier, inc=1, device_id=at(dz=d), device_id_type=MESH)

    pl.semaphore_wait(barrier, len(greet) + 15)

    def rows(half):
        return pl.ds(half * 256, 256)

    def shard(kind, dx, dy):
        xs, ys = lax.rem(x + 4 - dx, 4), lax.rem(y + 4 - dy, 4)
        return (lax.div(xs, 2) * 4 + ys) * 2 + (core if kind == "A" else sib)

    def acts_event(event):
        kind, dx, dy, half = event
        k = shard(kind, dx, dy)
        here = X.at[k, rows(half)]
        if (kind, dx, dy) == ("A", 0, 0):
            src = acts.at[rows(half)]
        else:
            wait(here, rx.at[k, half])
            src = here
        for way in onward(*event):
            ddx, ddy = STEPS[way]
            remote(src, here, sx.at[k, half, way], rx.at[k, half], at(dx=ddx, dy=ddy))

    def acts_sent(event):
        kind, dx, dy, half = event
        k = shard(kind, dx, dy)
        for way in onward(*event):
            wait(X.at[k, rows(half)], sx.at[k, half, way])

    def piece(kind, zz, j):
        j128 = pl.multiple_of(j * 128, 128)
        if kind == 0:
            return WKV.at[zz, pl.ds(j128, 128), :]
        if kind == 1:
            return WQ.at[zz, pl.ds(j128, 128), :]
        return WO.at[zz, :, pl.ds(j128, 128)]

    def kv_part(j, i):
        return WKV.at[z, pl.ds(pl.multiple_of(j * 128, 128), 128), pl.ds(pl.multiple_of(i * 128, 128), 128)]

    def zrow(d):
        return lax.rem(z - sgn * d + 32, 16)

    def local_copies():
        yield wkv, kv_part(xl, core), loc.at[0], None
        yield wq, piece(1, z, xl), loc.at[1], home
        yield wo, piece(2, z, xl), loc.at[2], home
        yield acts, X.at[zero], loc.at[3], home

    def when(cond, f):
        if cond is None:
            f()
        else:
            pl.when(cond)(f)

    for src, dst, sem, cond in local_copies():
        when(cond, lambda: pltpu.make_async_copy(src, dst, sem).start())

    @pl.when(away)
    def _():
        for half in (0, 1):
            remote(acts.at[rows(half)], X.at[zero, rows(half)], sd.at[half], rx.at[zero, half], at(to=sib))

    remote(wkv, kv_part(xl, core), s0.at[0], r0kv.at[xl, core], at(to=sib))
    remote(wkv, kv_part(xl, core), s0.at[1], r0kv.at[xl, core], at(dx=pdx))
    remote(wkv, kv_part(xl, core), s0.at[2], r0kv.at[xl, core], at(dx=pdx, to=sib))

    def share(src, kind, sem, slot):
        @pl.when(home)
        def _():
            remote(src, piece(kind, z, xl), s0.at[slot], sem.at[xl], at(to=sib))

        @pl.when(away)
        def _():
            remote(src, piece(kind, z, xl), s0.at[slot], sem.at[xl], at(dx=pdx))
            remote(src, piece(kind, z, xl), s0.at[slot + 1], sem.at[xl], at(dx=pdx, to=sib))

    remote(tmask, TMR, sm.at[0], rm.at[0], at(dx=pdx))
    remote(amask, AMR, sm.at[1], rm.at[1], at(dx=pdx))

    def z_own(kind):
        for j in (xl, 1 - xl):
            own = j is xl
            if kind == 0:
                if own:
                    pltpu.make_async_copy(wkv, kv_part(xl, core), loc.at[0]).wait()
                    wait(kv_part(xl, sib), r0kv.at[xl, sib])
                else:
                    wait(kv_part(j, 0), r0kv.at[j, 0])
                    wait(kv_part(j, 1), r0kv.at[j, 1])
            else:
                src, sem = ((wq, r0q), (wo, r0o))[kind - 1]
                if own:
                    pl.when(home)(lambda: pltpu.make_async_copy(src, piece(kind, z, xl), loc.at[kind]).wait())
                    pl.when(away)(lambda: wait(piece(kind, z, xl), sem.at[xl]))
                else:
                    wait(piece(kind, z, j), sem.at[j])
            remote(piece(kind, z, j), piece(kind, z, j), sz.at[kind, 0, j], rz.at[kind, 0, j], at(dz=sgn))

    def z_step(kind, d):
        zz = zrow(d)
        for j in (0, 1) if d < 8 else (core,):
            ref = piece(kind, zz, j)
            wait(ref, rz.at[kind, d - 1, j])
            if d < 7:
                remote(ref, ref, sz.at[kind, d, j], rz.at[kind, d, j], at(dz=sgn))
            remote(ref, ref, ss.at[kind, d - 1, j], rs.at[kind, d - 1, j], at(to=sib))
        if d == 7:
            ref = piece(kind, zz, core)
            remote(ref, ref, sz.at[kind, d, core], rz.at[kind, d, core], at(dz=sgn))

    def z_sent(kind):
        for d in range(8):
            for j in (0, 1) if d < 7 else (core,):
                wait(piece(kind, z, j), sz.at[kind, d, j])
        for d in range(1, 9):
            for j in (0, 1) if d < 8 else (core,):
                wait(piece(kind, z, j), ss.at[kind, d - 1, j])

    def z_sib(kind, d):
        for j in (0, 1) if d < 8 else (sib,):
            wait(piece(kind, zrow(-d), j), rs.at[kind, d - 1, j])

    def acts_events(lo, hi):
        @pl.when(home)
        def _():
            for event in ORDER_HOME[lo:hi]:
                acts_event(event)

        @pl.when(away)
        def _():
            for event in ORDER_AWAY[lo:hi]:
                acts_event(event)

    pl.when(home)(lambda: [acts_event(e) for e in ORDER_HOME[:2]] and None)
    share(wq, 1, r0q, 3)
    z_own(0)
    z_own(1)
    pl.when(home)(lambda: [acts_event(e) for e in ORDER_HOME[2:8]] and None)
    pl.when(away)(lambda: [acts_event(e) for e in ORDER_AWAY[:6]] and None)
    share(wo, 2, r0o, 5)
    cuts_home = [8, 13, 17, 20, 24, 28, 32]
    cuts_away = [6, 11, 16, 22, 25, 28, 32]
    for d in range(1, 7):
        z_step(0, d)
        z_step(1, d)
        lo, hi = cuts_home[d - 1], cuts_home[d]
        pl.when(home)(lambda: [acts_event(e) for e in ORDER_HOME[lo:hi]] and None)
        lo, hi = cuts_away[d - 1], cuts_away[d]
        pl.when(away)(lambda: [acts_event(e) for e in ORDER_AWAY[lo:hi]] and None)
    for d in (7, 8):
        z_step(0, d)
        z_step(1, d)
    z_own(2)
    pl.when(home)(lambda: pltpu.make_async_copy(acts, X.at[zero], loc.at[3]).wait())
    for d in range(1, 9):
        z_sib(0, d)
        z_sib(1, d)

    ACCQ[...] = jnp.zeros_like(ACCQ)
    ACCK[...] = jnp.zeros_like(ACCK)
    SSQ[...] = jnp.zeros_like(SSQ)

    @pl.loop(0, 16)
    def _(k):
        v = X[k].astype(F32)
        sq = v * v
        SSQ[...] += sq[:, :128] + sq[:, 128:]
        g = gain[:, pl.ds(pl.multiple_of(k * 256, 256), 256)].astype(F32)
        scaled = (v * g).astype(BF16)
        ACCQ[...] += jnp.dot(scaled, WQ[k], preferred_element_type=F32)
        ACCK[...] += jnp.dot(scaled, WKV[k], preferred_element_type=F32)

    inv = lax.rsqrt(jnp.sum(SSQ[...], -1, keepdims=True) * (1.0 / 4096) + 1e-5)
    block = 2 * z + core
    cb, sb = coff[pl.ds(block, 1), :], soff[pl.ds(block, 1), :]
    lane = lax.broadcasted_iota(jnp.int32, (1, 128), 1)
    cos = cb * ctab[...] - sb * stab[...]
    sin = sb * ctab[...] + cb * stab[...]
    sin = jnp.where(lane < 64, -sin, sin)

    def rope(v):
        return v * cos + pltpu.roll(v, 64, 1) * sin

    KV[:, :128] = rope(ACCK[:, :128] * inv).astype(BF16)
    KV[:, 128:] = (ACCK[:, 128:] * inv).astype(BF16)

    anchor = aidx[0]
    anchor_z, anchor_core = lax.div(anchor, 2), lax.rem(anchor, 2)
    mine = pl.ds(pl.multiple_of(core * 256, 256), 256)
    remote(KV.at[pl.ds(pl.multiple_of(sib * 256, 256), 256)], AB, sa, ra, at(to=sib))
    for h in (0, 1):
        q = (rope(ACCQ[:, h * 128:(h + 1) * 128] * inv) * (128 ** -0.5)).astype(BF16)
        for i in range(4):
            QB[i, h * 128:(h + 1) * 128, :] = q[i * 128:(i + 1) * 128]
    wait(AB, ra)
    CAND[...] = jnp.where(anchor_core == core, KV[mine, :], AB[...]).reshape(16, 16, 256)

    @pl.loop(1, 16)
    def _(s):
        d = lax.rem(s + 7, 15) + 1
        to = lax.rem(z + d, 16)
        remote(CAND.at[to], AR.at[z], sar.at[d], rar.at[z], at(dz=d))

    AR[z] = CAND[z]

    for ref, got, dst in ((tmask, TMR, BOWN), (amask, AMR, BFAR)):
        wait(got, rm.at[0 if ref is tmask else 1])
        seen = jnp.where(home, ref[0], got[0])
        if ref is amask:
            seen = jnp.where(block != anchor, seen, 0)
        term = jnp.where(seen == 1, 0.0, MASKED).astype(F32)
        for i in range(4):
            for j in range(4):
                dst[i, :, j * 128:(j + 1) * 128] = jnp.broadcast_to(term[i:i + 1, j:j + 1], (8, 128))

    over = (((1,), (1,)), ((), ()))
    row = lax.rem(lax.broadcasted_iota(jnp.int32, (256, 128), 0), 128)
    col = lax.broadcasted_iota(jnp.int32, (256, 128), 1)
    causal = jnp.where(col <= row, 0.0, MASKED).astype(F32)
    for i in range(4):
        n = (i + 1) * 128
        s = lax.dot_general(QB[i], KV[:n, :128], over, preferred_element_type=F32) + BOWN[i, 0:1, :n]
        last = s[:, n - 128:] + causal
        s = last if i == 0 else jnp.concatenate([s[:, :n - 128], last], 1)
        m = jnp.max(s, -1, keepdims=True)
        p = jnp.exp(s - m)
        MS[i] = jnp.broadcast_to(m, (256, 128))
        LS[i] = jnp.broadcast_to(jnp.sum(p, -1, keepdims=True), (256, 128))
        ACC[i] = jnp.dot(p.astype(BF16), KV[:n, 128:], preferred_element_type=F32)

    z_step(2, 1)
    z_step(2, 2)
    z_step(2, 3)

    @pl.loop(1, 16)
    def _(d):
        frm = lax.rem(z + d, 16)
        wait(AR.at[frm], rar.at[frm])

    SEL[...] = AR[anchor_z]

    @pl.loop(1, 16)
    def _(s):
        d = lax.rem(s + 7, 15) + 1
        remote(SEL, AKV.at[core, z], sak.at[d], rak.at[z], at(dz=d))

    AKV[core, z] = SEL[...]
    z_step(2, 4)
    z_step(2, 5)
    z_step(2, 6)

    @pl.loop(1, 16)
    def _(d):
        frm = lax.rem(z + d, 16)
        wait(AKV.at[core, frm], rak.at[frm])

    remote(AKV.at[core], AKV.at[core], sad, rad, at(to=sib))
    z_step(2, 7)
    z_step(2, 8)
    wait(AKV.at[sib], rad)
    far = AKV[...].reshape(512, 256)
    for i in range(4):
        s = lax.dot_general(QB[i], far[:, :128], over, preferred_element_type=F32) + BFAR[i, 0:1, :]
        m0 = MS[i][:, :1]
        m = jnp.maximum(m0, jnp.max(s, -1, keepdims=True))
        p = jnp.exp(s - m)
        alpha = jnp.exp(m0 - m)
        total = LS[i][:, :1] * alpha + jnp.sum(p, -1, keepdims=True)
        o = ACC[i] * alpha + jnp.dot(p.astype(BF16), far[:, 128:], preferred_element_type=F32)
        o = (o / total).astype(BF16)
        for h in (0, 1):
            ATT[i * 128:(i + 1) * 128, h * 128:(h + 1) * 128] = o[h * 128:(h + 1) * 128]

    offsets = [0]
    for d in range(1, 8):
        offsets += [d, -d]
    offsets += [8]

    def block_of(u, half):
        return lax.rem(z + offsets[2 * u + half] + 32, 16)

    y1, y2, y3 = lax.rem(y + 1, 4), lax.rem(y + 2, 4), lax.rem(y + 3, 4)
    hr = lax.div(lax.rem(x + 1, 4), 2)
    hl = lax.div(lax.rem(x + 3, 4), 2)

    class Unit:
        def __init__(self, u):
            self.u = u
            self.xfirst = u % 2 == 0

        def xs(self, half, h):
            return PB.at[self.u, half, h] if self.xfirst else PB.at[self.u, half, h, y]

        def rxs(self, way, half):
            return RX.at[self.u, way, half] if self.xfirst else RX.at[self.u, way, half, 0]

        def ys(self, half, yy):
            return PB.at[self.u, half, xh, yy] if self.xfirst else PB.at[self.u, half, :, yy]

        def ryc(self, way):
            return RYC.at[self.u, way, 0] if self.xfirst else RYC.at[self.u, way]

        def ryf(self, way, half):
            return RYF.at[self.u, way, half, 0] if self.xfirst else RYF.at[self.u, way, half]

        def sendx(self, src, slot, dx, way, half):
            remote(src, self.rxs(way, half), spx.at[self.u, slot], rpx.at[self.u, way, half], at(dx=dx))

        def sendyc(self, src, slot, dy, way):
            remote(src, self.ryc(way), spy.at[self.u, slot], rpyc.at[self.u, way], at(dy=dy))

        def sendyf(self, src, slot, dy, way, half):
            remote(src, self.ryf(way, half), spy.at[self.u, slot], rpyf.at[self.u, way, half], at(dy=dy))

        def project(self):
            for half in (0, 1):
                b = block_of(self.u, half)
                part = jnp.dot(ATT[...], WO[b], preferred_element_type=F32).astype(BF16)
                PB[self.u, half] = part.reshape(2, 4, 64, 256)

        def x_begin(self):
            @pl.when(home)
            def _():
                self.sendx(self.xs(0, 1 - xh), 0, 1, 0, 0)
                self.sendx(self.xs(1, 1 - xh), 1, -1, 1, 1)

            @pl.when(away)
            def _():
                self.sendx(self.xs(1, hr), 0, 1, 0, 1)
                self.sendx(self.xs(0, hl), 1, -1, 1, 0)

        def add(self, ref, got):
            ref[...] = (ref[...].astype(F32) + got[...].astype(F32)).astype(BF16)

        def x_mid(self):
            @pl.when(away)
            def _():
                wait(self.rxs(0, 0), rpx.at[self.u, 0, 0])
                self.add(self.xs(0, hr), self.rxs(0, 0))
                self.sendx(self.xs(0, hr), 2, 1, 0, 0)
                wait(self.rxs(1, 1), rpx.at[self.u, 1, 1])
                self.add(self.xs(1, hl), self.rxs(1, 1))
                self.sendx(self.xs(1, hl), 3, -1, 1, 1)

        def total(self, ref, one, two):
            return ref[...].astype(F32) + one[...].astype(F32) + two[...].astype(F32)

        def finish(self, half, value):
            value = value.astype(BF16)
            low, high = value[:32], value[32:]
            b = pl.multiple_of(block_of(self.u, half) * 256, 256)
            out[:, pl.ds(b, 256)] = jnp.where(core == 0, low, high)
            SB[self.u, half] = jnp.where(core == 0, high, low)
            if half == 1:
                remote(SB.at[self.u], OB.at[self.u], spd.at[self.u], rpd.at[self.u], at(to=sib))

        def x_end(self):
            @pl.when(home)
            def _():
                for half in (0, 1):
                    for way in (0, 1):
                        wait(self.rxs(way, half), rpx.at[self.u, way, half])
                    value = self.total(self.xs(half, xh), self.rxs(0, half), self.rxs(1, half))
                    if self.xfirst:
                        self.xs(half, xh)[...] = value.astype(BF16)
                    else:
                        self.finish(half, value)

        def on_y(self, f):
            if self.xfirst:
                pl.when(home)(f)
            else:
                f()

        def y_begin(self):
            def f():
                self.sendyc(self.ys(0, y2), 0, 1, 0)
                self.sendyc(self.ys(1, y2), 1, -1, 1)
                self.sendyf(self.ys(1, y1), 2, 1, 0, 1)
                self.sendyf(self.ys(0, y3), 3, -1, 1, 0)

            self.on_y(f)

        def y_mid(self):
            def f():
                wait(self.ryc(0), rpyc.at[self.u, 0])
                self.add(self.ys(0, y1), self.ryc(0))
                self.sendyf(self.ys(0, y1), 4, 1, 0, 0)
                wait(self.ryc(1), rpyc.at[self.u, 1])
                self.add(self.ys(1, y3), self.ryc(1))
                self.sendyf(self.ys(1, y3), 5, -1, 1, 1)

            self.on_y(f)

        def y_end(self):
            def f():
                for half in (0, 1):
                    for way in (0, 1):
                        wait(self.ryf(way, half), rpyf.at[self.u, way, half])
                    value = self.total(self.ys(half, y), self.ryf(0, half), self.ryf(1, half))
                    if self.xfirst:
                        self.finish(half, value)
                    else:
                        self.ys(half, y)[...] = value.astype(BF16)

            self.on_y(f)

        def stage(self, s):
            if s == 0:
                self.project()
            if self.xfirst:
                parts = [[self.x_begin], [self.x_mid], [self.x_end, self.y_begin], [self.y_mid], [self.y_end]]
            else:
                parts = [[self.y_begin], [self.y_mid], [self.y_end, self.x_begin], [self.x_mid], [self.x_end]]
            for part in parts[s]:
                part()

        def sent(self):
            @pl.when(home)
            def _():
                for slot in (0, 1):
                    wait(self.rxs(0, 0), spx.at[self.u, slot])
                wait(SB.at[self.u], spd.at[self.u])

            @pl.when(away)
            def _():
                for slot in range(4):
                    wait(self.rxs(0, 0), spx.at[self.u, slot])

            def f():
                for slot in range(6):
                    wait(self.ryc(0), spy.at[self.u, slot])

            self.on_y(f)

        def collect(self):
            @pl.when(away)
            def _():
                wait(OB.at[self.u], rpd.at[self.u])
                for half in (0, 1):
                    b = pl.multiple_of(block_of(self.u, half) * 256, 256)
                    out[:, pl.ds(b, 256)] = OB[self.u, half]

    for d in range(1, 9):
        z_sib(2, d)
    units = [Unit(u) for u in range(UNITS)]
    for t in range(UNITS + 4 * LAG):
        for s in reversed(range(5)):
            u = t - s * LAG
            if 0 <= u < UNITS:
                units[u].stage(s)

    pl.when(home)(lambda: [acts_sent(e) for e in ORDER_HOME] and None)
    pl.when(away)(lambda: [acts_sent(e) for e in ORDER_AWAY] and None)

    @pl.when(away)
    def _():
        for half in (0, 1):
            wait(X.at[0, rows(half)], sd.at[half])

    for slot in range(3):
        wait(kv_part(0, 0), s0.at[slot])
    for slot, kind in ((3, 1), (5, 2)):
        wait(piece(kind, z, 0), s0.at[slot])

        @pl.when(away)
        def _():
            wait(piece(kind, z, 0), s0.at[slot + 1])

    wait(TMR, sm.at[0])
    wait(AMR, sm.at[1])
    for kind in range(3):
        z_sent(kind)
    wait(AB, sa)

    @pl.loop(1, 16)
    def _(d):
        wait(SEL, sar.at[d])
        wait(SEL, sak.at[d])

    wait(AKV.at[0], sad)
    for unit in units:
        unit.sent()
    for unit in units:
        unit.collect()


def tables():
    f = 500000.0 ** (-np.arange(64, dtype=np.float64) * 2.0 / 128)
    f = np.concatenate([f, f])
    inner = np.arange(512, dtype=np.float64)[:, None] * f
    outer = 512.0 * np.arange(32, dtype=np.float64)[:, None] * f
    return [t.astype(np.float32) for t in (np.cos(inner), np.sin(inner), np.cos(outer), np.sin(outer))]


def local(activations, norm_gain, query_weight, kv_weight, out_weight, tile_mask, anchor_mask, anchor_index):
    vmem = pl.BlockSpec(memory_space=pltpu.VMEM)
    smem = pl.BlockSpec(memory_space=pltpu.SMEM)
    V = pltpu.VMEM
    D = pltpu.SemaphoreType.DMA
    scratch = [
        V((16, 512, 256), BF16), V((16, 256, 256), BF16), V((16, 256, 256), BF16), V((16, 256, 256), BF16),
        V((512, 256), F32), V((512, 256), F32), V((512, 128), F32),
        V((4, 256, 128), BF16), V((512, 256), BF16),
        V((1, 4, 4), jnp.int32), V((1, 4, 4), jnp.int32), V((4, 8, 512), F32), V((4, 8, 512), F32),
        V((256, 256), BF16), V((16, 16, 256), BF16), V((16, 16, 256), BF16), V((16, 256), BF16),
        V((2, 16, 16, 256), BF16), V((4, 256, 128), F32), V((4, 256, 128), F32), V((4, 256, 128), F32),
        V((512, 256), BF16),
        V((UNITS, 2, 2, 4, 64, 256), BF16), V((UNITS, 2, 2, 4, 64, 256), BF16),
        V((UNITS, 2, 2, 64, 256), BF16), V((UNITS, 2, 2, 2, 64, 256), BF16),
        V((UNITS, 2, 32, 256), BF16), V((UNITS, 2, 32, 256), BF16),
        D((16, 2)), D((16, 2, 4)), D((2,)), D((4,)), D((2, 2)), D((2,)), D((2,)), D((7,)),
        D((3, 8, 2)), D((3, 8, 2)), D((3, 8, 2)), D((3, 8, 2)), D((2,)), D((2,)),
        D(()), D(()), D((16,)), D((16,)), D((16,)), D((16,)), D(()), D(()),
        D((UNITS, 2, 2)), D((UNITS, 4)), D((UNITS, 2)), D((UNITS, 2, 2)), D((UNITS, 6)), D((UNITS,)), D((UNITS,)),
    ]
    return pl.pallas_call(
        body,
        out_shape=jax.ShapeDtypeStruct((32, 4096), BF16),
        in_specs=[vmem] * 7 + [smem] + [vmem] * 4,
        out_specs=vmem,
        scratch_shapes=scratch,
        compiler_params=pltpu.CompilerParams(
            collective_id=0, has_side_effects=True, vmem_limit_bytes=60 * 1024 * 1024
        ),
        name="star",
    )(
        activations, norm_gain.reshape(1, 4096), query_weight, kv_weight[:, 0, :], out_weight,
        tile_mask, anchor_mask, anchor_index, *[jnp.asarray(t) for t in tables()],
    )


def solution(mesh):
    placed = (
        P("ctx", "zero"), P(), P("ctx", "zero"), P("ctx", "zero", None), P("zero", "ctx"),
        P("ctx", None, None), P("ctx", None, None), P(),
    )
    return jax.shard_map(
        local, mesh=mesh, in_specs=placed, out_specs=P(("ctx", "zero"), None), check_vma=False
    )
```

time: 866 us -> 161 us (0.19)
  waiting for transfers between devices: 799 us -> 0 us
  Pallas kernels: 0 us -> 157 us
  starting transfers between devices: 24.6 us -> 0 us
  matrix products: 18.9 us -> 0 us
  between operations: 14.3 us -> 0.66 us
    all_gather x4 -> x0, waiting for transfers between devices: 412 us -> none  [the longest x1 127 us: local(): out_rows = lax.all_gather(out_weight, 'ctx', axis=1, tiled=True)]
    psum x1 -> x0, waiting for transfers between devices: 261 us -> none  [from_root(): return lax.psum(block, axis)]
    pallas_call x0 -> x1, Pallas kernels: none -> 157 us  [local(): pl.pallas_call(body, out_shape=jax.ShapeDtypeStruct((32, 4096), BF16), in...]
    reduce_scatter x1 -> x0, waiting for transfers between devices: 123 us -> none  [local(): lax.psum_scatter(jnp.dot(attended, out_rows, preferred_element_type=jnp.f...]
    ppermute x1 -> x0, starting transfers between devices: 24.4 us -> none  [from_partner(): return lax.ppermute(value, axis, pairs)]
    dot_general x4 -> x0, matrix products: 15.4 us -> none  [the longest x2 8.52 us: add_one(): return jnp.dot(normed, piece_rows, preferred_element_type=jnp.float32)]
  transfers between devices with their start and end apart: 7 -> 0, of which waited for: 7 -> 0; matrix products, arithmetic and copies ran while one was open for 3% -> 0% of each run, Pallas kernels for 0% -> 0%
where the time goes in v1:
time: 161 us
  Pallas kernels  157 us (98%)
  local copies, waits for them, and re-layouts  2.98 us (2%)
    pallas_call x1, Pallas kernels, local(): pl.pallas_call(body, out_shape=jax.ShapeDtypeStruct((32, 4096), BF16), in...  157 us

profile of v1, /device:TPU:1, one launch (start us, length us, event | category | flops | bytes accessed | tf_op | source)
XLA Modules:
  0.0 160.9 jit_solution(8285826631554375539)
XLA Ops:
  0.7 1.3 reshape.3.gain
  2.0 157.3 %star.1 = bf16[32,4096]{1,0:T(8,128)(2,1)} custom-call(bf16[512,256]{1,0:T(8,128)(2,1)} %acts.1, bf16[1,4096]{1,0:T(2,128)(2,1)} %reshape.3.gain, bf16[128,256]{1,0:T(8,128)(2,1)} %wq.1, bf16[128,128]{1,0:T(8,128)(2,1)} %bitcast.1, bf16[256,128]{1,0:T(8,128)(2,1)} %wo.1, s32[1,4,4]{2,1,0:T(4,128)} %tmask.1, s32[1,4,4]{2,1,0:T(4,128)} %amask.1, ...), custom_call_target="tpu_custom_call" | custom-call | tf_op jit(solution)/shard_map/star/pallas_call | solution.py:615
  159.3 1.7 %copy.15 = bf16[32,4096]{1,0:T(8,128)(2,1)} copy(bf16[32,4096]{1,0:T(8,128)(2,1)} %star.1) | data formatting | bytes 524288

commit v2 on v1

--- a/solution.py
+++ b/solution.py
@@ -14,7 +14,7 @@
 BF16 = jnp.bfloat16
 MASKED = -1e30
 UNITS = 8
-LAG = 1
+LAG = 3
 
 ORDER_HOME = [
     ("A", 0, 0, 0), ("A", 0, 0, 1), ("B", 0, 0, 0), ("B", 0, 0, 1), ("A", 0, 3, 0), ("A", 0, 1, 0),
@@ -57,9 +57,10 @@
 
 def body(
     acts, gain, wq, wkv, wo, tmask, amask, aidx, ctab, stab, coff, soff, out,
+    GAIN, CT, ST, CO, SO, AIDX, TM, AM,
     X, WQ, WKV, WO, ACCQ, ACCK, SSQ, QB, KV, TMR, AMR, BOWN, BFAR,
     AB, CAND, AR, SEL, AKV, MS, LS, ACC, ATT, PB, RX, RYC, RYF, SB, OB,
-    rx, sx, sd, loc, r0kv, r0q, r0o, s0, rz, sz, rs, ss, rm, sm,
+    ld, rx, sx, sd, loc, r0kv, r0q, r0o, s0, rz, sz, rs, ss, rm, sm,
     ra, sa, rar, sar, rak, sak, rad, sad,
     rpx, spx, rpyc, rpyf, spy, rpd, spd,
 ):
@@ -88,15 +89,19 @@
         pltpu.make_async_copy(ref, ref, sem).wait()
 
     barrier = pltpu.get_barrier_semaphore()
-    greet = [at(to=sib), at(dx=1), at(dx=-1), at(dx=pdx, to=sib), at(dy=1), at(dy=-1)]
+    greet = [at(to=sib), at(dx=1), at(dx=-1), at(dx=pdx, to=sib), at(dy=1), at(dy=-1), at(dz=1), at(dz=-1)]
     for dev in greet:
         pl.semaphore_signal(barrier, inc=1, device_id=dev, device_id_type=MESH)
 
-    @pl.loop(1, 16)
-    def _(d):
-        pl.semaphore_signal(barrier, inc=1, device_id=at(dz=d), device_id_type=MESH)
-
-    pl.semaphore_wait(barrier, len(greet) + 15)
+    loads = [
+        pltpu.make_async_copy(src, dst, ld.at[n])
+        for n, (src, dst) in enumerate(
+            [(gain, GAIN), (ctab, CT), (stab, ST), (coff, CO), (soff, SO), (aidx, AIDX), (tmask, TM), (amask, AM)]
+        )
+    ]
+    for copy in loads:
+        copy.start()
+    pl.semaphore_wait(barrier, len(greet))
 
     def rows(half):
         return pl.ds(half * 256, 256)
@@ -130,7 +135,7 @@
             return WKV.at[zz, pl.ds(j128, 128), :]
         if kind == 1:
             return WQ.at[zz, pl.ds(j128, 128), :]
-        return WO.at[zz, :, pl.ds(j128, 128)]
+        return WO.at[zz, j]
 
     def kv_part(j, i):
         return WKV.at[z, pl.ds(pl.multiple_of(j * 128, 128), 128), pl.ds(pl.multiple_of(i * 128, 128), 128)]
@@ -241,6 +246,10 @@
     for d in range(1, 7):
         z_step(0, d)
         z_step(1, d)
+        if d == 2:
+            z_own(2)
+        if d > 2:
+            z_step(2, d - 2)
         lo, hi = cuts_home[d - 1], cuts_home[d]
         pl.when(home)(lambda: [acts_event(e) for e in ORDER_HOME[lo:hi]] and None)
         lo, hi = cuts_away[d - 1], cuts_away[d]
@@ -248,12 +257,14 @@
     for d in (7, 8):
         z_step(0, d)
         z_step(1, d)
-    z_own(2)
+        z_step(2, d - 2)
     pl.when(home)(lambda: pltpu.make_async_copy(acts, X.at[zero], loc.at[3]).wait())
     for d in range(1, 9):
         z_sib(0, d)
         z_sib(1, d)
 
+    for copy in loads:
+        copy.wait()
     ACCQ[...] = jnp.zeros_like(ACCQ)
     ACCK[...] = jnp.zeros_like(ACCK)
     SSQ[...] = jnp.zeros_like(SSQ)
@@ -263,17 +274,17 @@
         v = X[k].astype(F32)
         sq = v * v
         SSQ[...] += sq[:, :128] + sq[:, 128:]
-        g = gain[:, pl.ds(pl.multiple_of(k * 256, 256), 256)].astype(F32)
+        g = GAIN[pl.ds(pl.multiple_of(k * 256, 256), 256)].astype(F32)[None, :]
         scaled = (v * g).astype(BF16)
         ACCQ[...] += jnp.dot(scaled, WQ[k], preferred_element_type=F32)
         ACCK[...] += jnp.dot(scaled, WKV[k], preferred_element_type=F32)
 
     inv = lax.rsqrt(jnp.sum(SSQ[...], -1, keepdims=True) * (1.0 / 4096) + 1e-5)
     block = 2 * z + core
-    cb, sb = coff[pl.ds(block, 1), :], soff[pl.ds(block, 1), :]
+    cb, sb = CO[pl.ds(block, 1), :], SO[pl.ds(block, 1), :]
     lane = lax.broadcasted_iota(jnp.int32, (1, 128), 1)
-    cos = cb * ctab[...] - sb * stab[...]
-    sin = sb * ctab[...] + cb * stab[...]
+    cos = cb * CT[...] - sb * ST[...]
+    sin = sb * CT[...] + cb * ST[...]
     sin = jnp.where(lane < 64, -sin, sin)
 
     def rope(v):
@@ -282,7 +293,7 @@
     KV[:, :128] = rope(ACCK[:, :128] * inv).astype(BF16)
     KV[:, 128:] = (ACCK[:, 128:] * inv).astype(BF16)
 
-    anchor = aidx[0]
+    anchor = AIDX[0]
     anchor_z, anchor_core = lax.div(anchor, 2), lax.rem(anchor, 2)
     mine = pl.ds(pl.multiple_of(core * 256, 256), 256)
     remote(KV.at[pl.ds(pl.multiple_of(sib * 256, 256), 256)], AB, sa, ra, at(to=sib))
@@ -301,10 +312,10 @@
 
     AR[z] = CAND[z]
 
-    for ref, got, dst in ((tmask, TMR, BOWN), (amask, AMR, BFAR)):
-        wait(got, rm.at[0 if ref is tmask else 1])
+    for ref, got, dst in ((TM, TMR, BOWN), (AM, AMR, BFAR)):
+        wait(got, rm.at[0 if ref is TM else 1])
         seen = jnp.where(home, ref[0], got[0])
-        if ref is amask:
+        if ref is AM:
             seen = jnp.where(block != anchor, seen, 0)
         term = jnp.where(seen == 1, 0.0, MASKED).astype(F32)
         for i in range(4):
@@ -326,9 +337,7 @@
         LS[i] = jnp.broadcast_to(jnp.sum(p, -1, keepdims=True), (256, 128))
         ACC[i] = jnp.dot(p.astype(BF16), KV[:n, 128:], preferred_element_type=F32)
 
-    z_step(2, 1)
-    z_step(2, 2)
-    z_step(2, 3)
+    z_step(2, 7)
 
     @pl.loop(1, 16)
     def _(d):
@@ -343,9 +352,7 @@
         remote(SEL, AKV.at[core, z], sak.at[d], rak.at[z], at(dz=d))
 
     AKV[core, z] = SEL[...]
-    z_step(2, 4)
-    z_step(2, 5)
-    z_step(2, 6)
+    z_step(2, 8)
 
     @pl.loop(1, 16)
     def _(d):
@@ -353,8 +360,6 @@
         wait(AKV.at[core, frm], rak.at[frm])
 
     remote(AKV.at[core], AKV.at[core], sad, rad, at(to=sib))
-    z_step(2, 7)
-    z_step(2, 8)
     wait(AKV.at[sib], rad)
     far = AKV[...].reshape(512, 256)
     for i in range(4):
@@ -413,7 +418,8 @@
         def project(self):
             for half in (0, 1):
                 b = block_of(self.u, half)
-                part = jnp.dot(ATT[...], WO[b], preferred_element_type=F32).astype(BF16)
+                w = jnp.concatenate([WO[b, 0], WO[b, 1]], 1)
+                part = jnp.dot(ATT[...], w, preferred_element_type=F32).astype(BF16)
                 PB[self.u, half] = part.reshape(2, 4, 64, 256)
 
         def x_begin(self):
@@ -593,11 +599,12 @@
 
 def local(activations, norm_gain, query_weight, kv_weight, out_weight, tile_mask, anchor_mask, anchor_index):
     vmem = pl.BlockSpec(memory_space=pltpu.VMEM)
-    smem = pl.BlockSpec(memory_space=pltpu.SMEM)
     V = pltpu.VMEM
     D = pltpu.SemaphoreType.DMA
     scratch = [
-        V((16, 512, 256), BF16), V((16, 256, 256), BF16), V((16, 256, 256), BF16), V((16, 256, 256), BF16),
+        V((4096,), BF16), V((512, 128), F32), V((512, 128), F32), V((32, 128), F32), V((32, 128), F32),
+        pltpu.SMEM((1,), jnp.int32), V((1, 4, 4), jnp.int32), V((1, 4, 4), jnp.int32),
+        V((16, 512, 256), BF16), V((16, 256, 256), BF16), V((16, 256, 256), BF16), V((16, 2, 256, 128), BF16),
         V((512, 256), F32), V((512, 256), F32), V((512, 128), F32),
         V((4, 256, 128), BF16), V((512, 256), BF16),
         V((1, 4, 4), jnp.int32), V((1, 4, 4), jnp.int32), V((4, 8, 512), F32), V((4, 8, 512), F32),
@@ -607,6 +614,7 @@
         V((UNITS, 2, 2, 4, 64, 256), BF16), V((UNITS, 2, 2, 4, 64, 256), BF16),
         V((UNITS, 2, 2, 64, 256), BF16), V((UNITS, 2, 2, 2, 64, 256), BF16),
         V((UNITS, 2, 32, 256), BF16), V((UNITS, 2, 32, 256), BF16),
+        D((8,)),
         D((16, 2)), D((16, 2, 4)), D((2,)), D((4,)), D((2, 2)), D((2,)), D((2,)), D((7,)),
         D((3, 8, 2)), D((3, 8, 2)), D((3, 8, 2)), D((3, 8, 2)), D((2,)), D((2,)),
         D(()), D(()), D((16,)), D((16,)), D((16,)), D((16,)), D(()), D(()),
@@ -615,7 +623,7 @@
     return pl.pallas_call(
         body,
         out_shape=jax.ShapeDtypeStruct((32, 4096), BF16),
-        in_specs=[vmem] * 7 + [smem] + [vmem] * 4,
+        in_specs=[pl.BlockSpec(memory_space=pl.ANY)] * 12,
         out_specs=vmem,
         scratch_shapes=scratch,
         compiler_params=pltpu.CompilerParams(
@@ -623,7 +631,7 @@
         ),
         name="star",
     )(
-        activations, norm_gain.reshape(1, 4096), query_weight, kv_weight[:, 0, :], out_weight,
+        activations, norm_gain, query_weight, kv_weight[:, 0, :], out_weight,
         tile_mask, anchor_mask, anchor_index, *[jnp.asarray(t) for t in tables()],
     )
 

time: 161 us -> 127 us (0.79)
  Pallas kernels: 157 us -> 125 us
    pallas_call x1, Pallas kernels: 157 us -> 125 us  [local(): pl.pallas_call(body, out_shape=jax.ShapeDtypeStruct((32, 4096), BF16), in...]
where the time goes in v2:
time: 127 us
  Pallas kernels  125 us (98%)
  local copies, waits for them, and re-layouts  1.67 us (1%)
    pallas_call x1, Pallas kernels, local(): pl.pallas_call(body, out_shape=jax.ShapeDtypeStruct((32, 4096), BF16), in...  125 us

profile of v2, /device:TPU:1, one launch (start us, length us, event | category | flops | bytes accessed | tf_op | source)
XLA Modules:
  0.0 126.9 jit_solution(1142886254084338638)
XLA Ops:
  0.7 124.6 %star.1 = bf16[32,4096]{1,0:T(8,128)(2,1)} custom-call(bf16[512,256]{1,0:T(8,128)(2,1)} %acts.1, bf16[4096]{0:T(1024)(128)(2,1)} %gain.1, bf16[128,256]{1,0:T(8,128)(2,1)} %wq.1, bf16[128,128]{1,0:T(8,128)(2,1)} %bitcast.1, bf16[256,128]{1,0:T(8,128)(2,1)} %wo.1, s32[1,4,4]{2,1,0:T(4,128)} %tmask.1, s32[1,4,4]{2,1,0:T(4,128)} %amask.1, s32[1]{0:T(128)S(6)} %copy.14.aidx, ...), custom_call_target="tpu_custom_call" | custom-call | tf_op jit(solution)/shard_map/star/pallas_call | solution.py:623
  125.3 1.7 %copy.15 = bf16[32,4096]{1,0:T(8,128)(2,1)} copy(bf16[32,4096]{1,0:T(8,128)(2,1)} %star.1) | data formatting | bytes 524288

commit v3 on v2

--- a/solution.py
+++ b/solution.py
@@ -14,7 +14,7 @@
 BF16 = jnp.bfloat16
 MASKED = -1e30
 UNITS = 8
-LAG = 3
+LAG = 4
 
 ORDER_HOME = [
     ("A", 0, 0, 0), ("A", 0, 0, 1), ("B", 0, 0, 0), ("B", 0, 0, 1), ("A", 0, 3, 0), ("A", 0, 1, 0),
@@ -58,7 +58,7 @@
 def body(
     acts, gain, wq, wkv, wo, tmask, amask, aidx, ctab, stab, coff, soff, out,
     GAIN, CT, ST, CO, SO, AIDX, TM, AM,
-    X, WQ, WKV, WO, ACCQ, ACCK, SSQ, QB, KV, TMR, AMR, BOWN, BFAR,
+    X, XG, WQ, WKV, WO, ACCQ, ACCK, SSQ, QB, KV, TMR, AMR, BOWN, BFAR,
     AB, CAND, AR, SEL, AKV, MS, LS, ACC, ATT, PB, RX, RYC, RYF, SB, OB,
     ld, rx, sx, sd, loc, r0kv, r0q, r0o, s0, rz, sz, rs, ss, rm, sm,
     ra, sa, rar, sar, rak, sak, rad, sad,
@@ -246,10 +246,10 @@
     for d in range(1, 7):
         z_step(0, d)
         z_step(1, d)
-        if d == 2:
+        if d == 4:
             z_own(2)
-        if d > 2:
-            z_step(2, d - 2)
+        if d > 4:
+            z_step(2, d - 4)
         lo, hi = cuts_home[d - 1], cuts_home[d]
         pl.when(home)(lambda: [acts_event(e) for e in ORDER_HOME[lo:hi]] and None)
         lo, hi = cuts_away[d - 1], cuts_away[d]
@@ -257,7 +257,7 @@
     for d in (7, 8):
         z_step(0, d)
         z_step(1, d)
-        z_step(2, d - 2)
+        z_step(2, d - 4)
     pl.when(home)(lambda: pltpu.make_async_copy(acts, X.at[zero], loc.at[3]).wait())
     for d in range(1, 9):
         z_sib(0, d)
@@ -276,7 +276,7 @@
         SSQ[...] += sq[:, :128] + sq[:, 128:]
         g = GAIN[pl.ds(pl.multiple_of(k * 256, 256), 256)].astype(F32)[None, :]
         scaled = (v * g).astype(BF16)
-        ACCQ[...] += jnp.dot(scaled, WQ[k], preferred_element_type=F32)
+        XG[k] = scaled
         ACCK[...] += jnp.dot(scaled, WKV[k], preferred_element_type=F32)
 
     inv = lax.rsqrt(jnp.sum(SSQ[...], -1, keepdims=True) * (1.0 / 4096) + 1e-5)
@@ -297,10 +297,6 @@
     anchor_z, anchor_core = lax.div(anchor, 2), lax.rem(anchor, 2)
     mine = pl.ds(pl.multiple_of(core * 256, 256), 256)
     remote(KV.at[pl.ds(pl.multiple_of(sib * 256, 256), 256)], AB, sa, ra, at(to=sib))
-    for h in (0, 1):
-        q = (rope(ACCQ[:, h * 128:(h + 1) * 128] * inv) * (128 ** -0.5)).astype(BF16)
-        for i in range(4):
-            QB[i, h * 128:(h + 1) * 128, :] = q[i * 128:(i + 1) * 128]
     wait(AB, ra)
     CAND[...] = jnp.where(anchor_core == core, KV[mine, :], AB[...]).reshape(16, 16, 256)
 
@@ -312,6 +308,14 @@
 
     AR[z] = CAND[z]
 
+    @pl.loop(0, 16)
+    def _(k):
+        ACCQ[...] += jnp.dot(XG[k], WQ[k], preferred_element_type=F32)
+
+    for h in (0, 1):
+        q = (rope(ACCQ[:, h * 128:(h + 1) * 128] * inv) * (128 ** -0.5)).astype(BF16)
+        for i in range(4):
+            QB[i, h * 128:(h + 1) * 128, :] = q[i * 128:(i + 1) * 128]
     for ref, got, dst in ((TM, TMR, BOWN), (AM, AMR, BFAR)):
         wait(got, rm.at[0 if ref is TM else 1])
         seen = jnp.where(home, ref[0], got[0])
@@ -337,7 +341,8 @@
         LS[i] = jnp.broadcast_to(jnp.sum(p, -1, keepdims=True), (256, 128))
         ACC[i] = jnp.dot(p.astype(BF16), KV[:n, 128:], preferred_element_type=F32)
 
-    z_step(2, 7)
+    z_step(2, 5)
+    z_step(2, 6)
 
     @pl.loop(1, 16)
     def _(d):
@@ -352,7 +357,7 @@
         remote(SEL, AKV.at[core, z], sak.at[d], rak.at[z], at(dz=d))
 
     AKV[core, z] = SEL[...]
-    z_step(2, 8)
+    z_step(2, 7)
 
     @pl.loop(1, 16)
     def _(d):
@@ -545,10 +550,14 @@
                     b = pl.multiple_of(block_of(self.u, half) * 256, 256)
                     out[:, pl.ds(b, 256)] = OB[self.u, half]
 
-    for d in range(1, 9):
-        z_sib(2, d)
     units = [Unit(u) for u in range(UNITS)]
+    seen = 0
     for t in range(UNITS + 4 * LAG):
+        if seen < 8:
+            seen += 1
+            if seen == 4:
+                z_step(2, 8)
+            z_sib(2, seen)
         for s in reversed(range(5)):
             u = t - s * LAG
             if 0 <= u < UNITS:
@@ -604,7 +613,7 @@
     scratch = [
         V((4096,), BF16), V((512, 128), F32), V((512, 128), F32), V((32, 128), F32), V((32, 128), F32),
         pltpu.SMEM((1,), jnp.int32), V((1, 4, 4), jnp.int32), V((1, 4, 4), jnp.int32),
-        V((16, 512, 256), BF16), V((16, 256, 256), BF16), V((16, 256, 256), BF16), V((16, 2, 256, 128), BF16),
+        V((16, 512, 256), BF16), V((16, 512, 256), BF16), V((16, 256, 256), BF16), V((16, 256, 256), BF16), V((16, 2, 256, 128), BF16),
         V((512, 256), F32), V((512, 256), F32), V((512, 128), F32),
         V((4, 256, 128), BF16), V((512, 256), BF16),
         V((1, 4, 4), jnp.int32), V((1, 4, 4), jnp.int32), V((4, 8, 512), F32), V((4, 8, 512), F32),

time: 127 us -> 124 us (0.976)
  Pallas kernels: 125 us -> 121 us
    pallas_call x1, Pallas kernels: 125 us -> 121 us  [local(): pl.pallas_call(body, out_shape=jax.ShapeDtypeStruct((32, 4096), BF16), in...]
where the time goes in v3:
time: 124 us
  Pallas kernels  121 us (98%)
  local copies, waits for them, and re-layouts  1.67 us (1%)
    pallas_call x1, Pallas kernels, local(): pl.pallas_call(body, out_shape=jax.ShapeDtypeStruct((32, 4096), BF16), in...  121 us

profile of v3, /device:TPU:1, one launch (start us, length us, event | category | flops | bytes accessed | tf_op | source)
XLA Modules:
  0.0 123.7 jit_solution(11409044693547346848)
XLA Ops:
  0.7 121.3 %star.1 = bf16[32,4096]{1,0:T(8,128)(2,1)} custom-call(bf16[512,256]{1,0:T(8,128)(2,1)} %acts.1, bf16[4096]{0:T(1024)(128)(2,1)} %gain.1, bf16[128,256]{1,0:T(8,128)(2,1)} %wq.1, bf16[128,128]{1,0:T(8,128)(2,1)} %bitcast.1, bf16[256,128]{1,0:T(8,128)(2,1)} %wo.1, s32[1,4,4]{2,1,0:T(4,128)} %tmask.1, s32[1,4,4]{2,1,0:T(4,128)} %amask.1, s32[1]{0:T(128)S(6)} %copy.14.aidx, ...), custom_call_target="tpu_custom_call" | custom-call | tf_op jit(solution)/shard_map/star/pallas_call | solution.py:632
  122.0 1.7 %copy.15 = bf16[32,4096]{1,0:T(8,128)(2,1)} copy(bf16[32,4096]{1,0:T(8,128)(2,1)} %star.1) | data formatting | bytes 524288

commit v4 on v3

--- a/solution.py
+++ b/solution.py
@@ -241,9 +241,9 @@
     pl.when(home)(lambda: [acts_event(e) for e in ORDER_HOME[2:8]] and None)
     pl.when(away)(lambda: [acts_event(e) for e in ORDER_AWAY[:6]] and None)
     share(wo, 2, r0o, 5)
-    cuts_home = [8, 13, 17, 20, 24, 28, 32]
-    cuts_away = [6, 11, 16, 22, 25, 28, 32]
-    for d in range(1, 7):
+    cuts_home = [8, 12, 15, 18, 20, 24, 27, 32]
+    cuts_away = [6, 10, 14, 18, 22, 25, 28, 32]
+    for d in range(1, 8):
         z_step(0, d)
         z_step(1, d)
         if d == 4:
@@ -254,7 +254,7 @@
         pl.when(home)(lambda: [acts_event(e) for e in ORDER_HOME[lo:hi]] and None)
         lo, hi = cuts_away[d - 1], cuts_away[d]
         pl.when(away)(lambda: [acts_event(e) for e in ORDER_AWAY[lo:hi]] and None)
-    for d in (7, 8):
+    for d in (8,):
         z_step(0, d)
         z_step(1, d)
         z_step(2, d - 4)

time: 124 us -> 122 us (0.984)
  Pallas kernels: 121 us -> 119 us
    pallas_call x1, Pallas kernels: 121 us -> 119 us  [local(): pl.pallas_call(body, out_shape=jax.ShapeDtypeStruct((32, 4096), BF16), in...]
where the time goes in v4:
time: 122 us; the launch traced here: 121 us
  Pallas kernels  119 us (98%)
  local copies, waits for them, and re-layouts  1.67 us (1%)
    pallas_call x1, Pallas kernels, local(): pl.pallas_call(body, out_shape=jax.ShapeDtypeStruct((32, 4096), BF16), in...  119 us

profile of v4, /device:TPU:1, one launch (start us, length us, event | category | flops | bytes accessed | tf_op | source)
XLA Modules:
  0.0 121.5 jit_solution(1611650749372609927)
XLA Ops:
  0.7 119.1 %star.1 = bf16[32,4096]{1,0:T(8,128)(2,1)} custom-call(bf16[512,256]{1,0:T(8,128)(2,1)} %acts.1, bf16[4096]{0:T(1024)(128)(2,1)} %gain.1, bf16[128,256]{1,0:T(8,128)(2,1)} %wq.1, bf16[128,128]{1,0:T(8,128)(2,1)} %bitcast.1, bf16[256,128]{1,0:T(8,128)(2,1)} %wo.1, s32[1,4,4]{2,1,0:T(4,128)} %tmask.1, s32[1,4,4]{2,1,0:T(4,128)} %amask.1, s32[1]{0:T(128)S(6)} %copy.14.aidx, ...), custom_call_target="tpu_custom_call" | custom-call | tf_op jit(solution)/shard_map/star/pallas_call | solution.py:632
  119.8 1.7 %copy.15 = bf16[32,4096]{1,0:T(8,128)(2,1)} copy(bf16[32,4096]{1,0:T(8,128)(2,1)} %star.1) | data formatting | bytes 524288
